TPU v7x, 256 devices: a whole 4x4x8 slice. The times are simulated.
256 devices in a mesh: role: 2 (over core), exp: 8 (over z), tp: 16 (over x, y).
Axes of the slice: x: 4, y: 4, z: 8, core: 2. Of those that a mesh axis runs over, the one named last changes fastest.
Arguments:
- residual_in: bfloat16 [2048, 8192], P(('role', 'exp', 'tp')), may hold values from -64 to 64
- context: bfloat16 [2048, 8192], P(('role', 'exp'), 'tp'), may hold values from -6 to 6
- out_weight: bfloat16 [8192, 8192], P('tp', ('role', 'exp')), may hold values from -0.0625 to 0.0625
- norm_gain: bfloat16 [8192], replicated, may hold values from 0.5 to 1.5
- router: bfloat16 [2, 4, 8192], replicated, may hold values from -0.125 to 0.125
- up_weight: bfloat16 [2, 8, 8192, 6144], P('role', 'exp', None, 'tp'), may hold values from -0.0625 to 0.0625
- down_weight: bfloat16 [2, 8, 6144, 8192], P('role', 'exp', 'tp'), may hold values from -0.109375 to 0.109375
- modality: int32 [2048], P(('role', 'exp', 'tp')), may hold values from 0 to 1
- expert: int32 [2048], P(('role', 'exp', 'tp')), may hold values from 0 to 3, as said below
Outputs:
- mixed: bfloat16 [2048, 8192], P(('role', 'exp', 'tp'))
Inputs may be any that keep to these rules, and one draw needn't show every extreme that they name: Among the 8 tokens of one device at most 2 choose one expert of one modality, and in every device's tokens some expert of some modality is chosen by exactly 2.
All inputs are finite; a program needn't handle non-finite values.
Results may differ from a plain program's by a relative error of at most 0.0052.
Values may be sent and summed in bfloat16 or wider, within the bound.
A program may use at most 128 MiB of HBM per device.

v0:
```python
import jax
import jax.numpy as jnp
from jax import lax
from jax.sharding import PartitionSpec as P

EXPERTS = 4
CAP = 2
EPSILON = 1e-05


def in_blocks(array, dim, length):
    before, after = (array.shape[:dim], array.shape[dim + 1 :])
    return jnp.moveaxis(array.reshape(*before, length, -1, *after), dim, 0)


def summed_on_arrival(array, axis, dim):
    length = lax.axis_size(axis)
    blocks = lax.all_to_all(in_blocks(array, dim, length), axis, 0, 0, tiled=True)
    return jnp.sum(blocks, axis=0)


def in_order(blocks, dim):
    blocks = jnp.moveaxis(blocks, 0, dim)
    dims = blocks.shape
    return blocks.reshape(*dims[:dim], dims[dim] * dims[dim + 1], *dims[dim + 2 :])


def joined_exchange(array, axis, axes, splits, concats):
    sizes = [lax.axis_size(a) for a in axes]
    blocks = in_blocks(array, splits[0], sizes[0])
    blocks = jnp.moveaxis(in_blocks(blocks, splits[1] + 1, sizes[1]), 0, 1)
    inside = blocks.shape[2:]
    blocks = blocks.reshape(-1, *inside)
    blocks = lax.all_to_all(blocks, axis, split_axis=0, concat_axis=0, tiled=True)
    blocks = in_order(blocks.reshape(*sizes, *inside), concats[0] + 1)
    return in_order(blocks, concats[1])


def per_device(
    residual_in, context, out_weight, norm_gain, router, up_weight, down_weight, modality, expert
):
    tok_rows, width = residual_in.shape
    head_cols = context.shape[1]
    tp_count = lax.axis_size("tp")
    group_count = lax.axis_size("role") * lax.axis_size("exp")
    exp_count = lax.axis_size("exp")
    halves = exp_count // EXPERTS
    grouped = context.reshape(tp_count, tok_rows, head_cols)
    all_rows = lax.all_gather(grouped, ("role", "exp"), axis=1, tiled=True)
    all_rows = all_rows.reshape(tp_count * group_count * tok_rows, head_cols)
    partial_cols = summed_on_arrival(
        jnp.dot(all_rows, out_weight, preferred_element_type=jnp.float32), "tp", 0
    )
    projected = lax.all_to_all(
        partial_cols.reshape(group_count, tok_rows, out_weight.shape[1]),
        ("role", "exp"),
        split_axis=0,
        concat_axis=2,
        tiled=True,
    ).reshape(tok_rows, width)
    resid = (residual_in.astype(jnp.float32) + projected).astype(jnp.bfloat16)
    resid = lax.optimization_barrier(resid)
    widened = resid.astype(jnp.float32)
    inverse_rms = lax.rsqrt(jnp.mean(widened * widened, axis=-1, keepdims=True) + EPSILON)
    normed = (widened * inverse_rms * norm_gain.astype(jnp.float32)).astype(jnp.bfloat16)
    routes = modality * EXPERTS + expert
    choices_hot = routes[:, None] == jnp.arange(2 * EXPERTS, dtype=jnp.int32)[None, :]
    hot_ints = choices_hot.astype(jnp.int32)
    earlier = jnp.cumsum(hot_ints, axis=0) - hot_ints
    position = jnp.sum(earlier * hot_ints, axis=1)
    target = routes * CAP + position
    placed = (jnp.arange(2 * EXPERTS * CAP, dtype=jnp.int32)[:, None] == target[None, :]).astype(
        jnp.bfloat16
    )
    placed = placed.reshape(2, EXPERTS, CAP, tok_rows)
    logits = lax.dot_general(
        normed,
        router.reshape(2 * EXPERTS, width),
        (((1,), (1,)), ((), ())),
        preferred_element_type=jnp.float32,
    )
    gating = jax.nn.sigmoid(jnp.sum(jnp.where(choices_hot, logits, 0.0), axis=1))
    slotted = jnp.einsum("mecq,qd->mecd", placed, normed, preferred_element_type=jnp.float32)
    slotted = slotted.astype(jnp.bfloat16)
    outgoing = jnp.broadcast_to(slotted[:, :, None], (2, EXPERTS, halves, CAP, width))
    outgoing = outgoing.reshape(2, exp_count, CAP, width)
    incoming = joined_exchange(outgoing, ("role", "exp"), ("role", "exp"), (0, 1), (0, 1))
    local_slots = incoming.reshape(2 * exp_count * CAP, width)
    up_matrix = up_weight[0, 0]
    down_matrix = down_weight[0, 0]
    up_sums = jnp.dot(
        lax.all_gather(local_slots, "tp", axis=0, tiled=True),
        up_matrix,
        preferred_element_type=jnp.float32,
    )
    hidden = jax.nn.gelu(up_sums).astype(jnp.bfloat16)
    results = lax.psum_scatter(
        jnp.dot(hidden, down_matrix, preferred_element_type=jnp.float32),
        "tp",
        scatter_dimension=0,
        tiled=True,
    )
    returned = joined_exchange(
        results.reshape(2, exp_count, CAP, width).astype(jnp.bfloat16),
        ("role", "exp"),
        ("role", "exp"),
        (0, 1),
        (0, 1),
    ).astype(jnp.float32)
    expert_out = jnp.einsum(
        "mecq,mescd->qd",
        placed.astype(jnp.float32),
        returned.reshape(2, EXPERTS, halves, CAP, width),
        precision=lax.Precision.HIGHEST,
    )
    return (widened + gating[:, None] * expert_out).astype(jnp.bfloat16)


def solution(mesh):
    in_specs = (
        P(("role", "exp", "tp"), None),
        P(("role", "exp"), "tp"),
        P("tp", ("role", "exp")),
        P(),
        P(),
        P("role", "exp", None, "tp"),
        P("role", "exp", "tp", None),
        P(("role", "exp", "tp")),
        P(("role", "exp", "tp")),
    )
    out_specs = P(("role", "exp", "tp"), None)
    return jax.shard_map(
        per_device, mesh=mesh, in_specs=in_specs, out_specs=out_specs, check_vma=False
    )
```

profile of v0, /device:TPU:32, one launch (start us, length us, event | category | flops | bytes accessed | tf_op | source)
XLA Modules:
  0.0 412.4 jit_solution(11668320973444184488)
XLA Ops:
  6.5 0.7 all-gather.3.cloned.1.call-update
  7.3 43.4 %all-gather.3.cloned.1.call-done = bf16[16,128,512]{2,1,0:T(8,128)(2,1)} async-done(((bf16[16,8,512]{2,1,0:T(8,128)(2,1)}), bf16[16,128,512]{2,1,0:T(8,128)(2,1)}) %all-gather.3.cloned.1.call-update) | async-done | bytes 2097168 | tf_op jit(solution)/shard_map/all_gather | solution.py:49
  50.6 4.8 %fusion.20 = f32[16,128,512]{2,1,0:T(8,128)} fusion(bf16[16,128,512]{2,1,0:T(8,128)(2,1)} %all-gather.3.cloned.1.call-done, bf16[512,512]{1,0:T(8,128)(2,1)S(1)} %copy-done), kind=kOutput, calls=%fused_computation.21 | convolution fusion | flops 1073741824 | bytes 6815744 | tf_op jit(solution)/shard_map/dot_general | solution.py:52
  55.4 7.0 %all-to-all-start = ((f32[16,128,512]{2,1,0:T(8,128)}), f32[16,128,512]{2,1,0:T(8,128)}, u32[]{:S(2)}, u32[]{:S(2)}) async-start(f32[16,128,512]{2,1,0:T(8,128)} %fusion.20), calls=%async_computation | async-start | bytes 8388608 | tf_op jit(solution)/shard_map/all_to_all | solution.py:18
  62.5 56.5 %all-to-all-done = f32[16,128,512]{2,1,0:T(8,128)} async-done(((f32[16,128,512]{2,1,0:T(8,128)}), f32[16,128,512]{2,1,0:T(8,128)}, u32[]{:S(2)}, u32[]{:S(2)}) %all-to-all-start) | async-done | bytes 4194336 | tf_op jit(solution)/shard_map/all_to_all | solution.py:18
  119.0 3.3 reduce_sum.45
  122.3 4.9 %all-to-all-start.1 = ((f32[16,8,512]{2,1,0:T(8,128)}), f32[16,8,512]{2,1,0:T(8,128)S(1)}, u32[]{:S(2)}, u32[]{:S(2)}) async-start(f32[16,8,512]{2,1,0:T(8,128)} %bitcast.2), calls=%async_computation.1 | async-start | bytes 524288 | tf_op jit(solution)/shard_map/all_to_all | solution.py:54
  127.4 10.6 %all-to-all-done.1 = f32[16,8,512]{2,1,0:T(8,128)S(1)} async-done(((f32[16,8,512]{2,1,0:T(8,128)}), f32[16,8,512]{2,1,0:T(8,128)S(1)}, u32[]{:S(2)}, u32[]{:S(2)}) %all-to-all-start.1) | async-done | bytes 262176 | tf_op jit(solution)/shard_map/all_to_all | solution.py:54
  138.3 0.3 convolution_convert_fusion
  138.6 0.3 copy.13
  138.9 0.4 broadcast_in_dim.6
  139.3 19.8 %all_to_all.30 = bf16[16,1,1,2,8192]{4,3,2,1,0:T(2,128)(2,1)S(1)} all-to-all(bf16[16,1,1,2,8192]{4,3,2,1,0:T(2,128)(2,1)S(1)} %bitcast.64), channel_id=1, replica_groups=mesh['role'=2,'exp'=8,'tp'=16] {'role','exp'}, dimensions={0} | all-to-all | bytes 1048576 | tf_op jit(solution)/shard_map/all_to_all | solution.py:34
  159.1 1.0 reshape_reshape.3
  160.2 80.9 %all-gather.5.cloned.1.call-done = bf16[512,8192]{1,0:T(8,128)(2,1)} async-done(((bf16[32,8192]{1,0:T(8,128)(2,1)}), bf16[512,8192]{1,0:T(8,128)(2,1)}) %all-gather.5.cloned.1.call-update) | async-done | bytes 8388624 | tf_op jit(solution)/shard_map/all_gather | solution.py:92
  241.0 9.8 %fusion.17 = bf16[512,384]{1,0:T(8,128)(2,1)S(1)} fusion(bf16[512,8192]{1,0:T(8,128)(2,1)} %all-gather.5.cloned.1.call-done, bf16[1,1,8192,384]{3,2,1,0:T(8,128)(2,1)} %param.14), kind=kOutput, calls=%fused_computation.20 | convolution fusion | flops 3222994944 | bytes 15073280 | tf_op jit(solution)/shard_map/dot_general | solution.py:91
  250.8 10.9 %fusion.3 = f32[512,8192]{1,0:T(8,128)} fusion(bf16[512,384]{1,0:T(8,128)(2,1)S(1)} %fusion.17, bf16[1,1,384,8192]{3,2,1,0:T(8,128)(2,1)} %param.15), kind=kOutput, calls=%fused_computation.5 | convolution fusion | flops 3221225472 | bytes 23461888 | tf_op jit(solution)/shard_map/dot_general | solution.py:98
  261.7 115.6 %reduce-scatter.2.cloned.1.call-done = f32[32,8192]{1,0:T(8,128)} async-done(((f32[512,8192]{1,0:T(8,128)}), f32[32,8192]{1,0:T(8,128)}) %reduce-scatter.2.cloned.1.call-update) | async-done | bytes 1048592 | tf_op jit(solution)/shard_map/reduce_scatter | solution.py:97
  377.4 1.3 convert_element_type.70
  378.7 1.1 convert_element_type.71
  379.8 7.6 %all-to-all-start.3 = ((bf16[16,1,1,2,8192]{4,3,2,1,0:T(2,128)(2,1)}), bf16[16,1,1,2,8192]{4,3,2,1,0:T(2,128)(2,1)S(1)}, u32[]{:S(2)}, u32[]{:S(2)}) async-start(bf16[16,1,1,2,8192]{4,3,2,1,0:T(2,128)(2,1)} %bitcast.15), calls=%async_computation.4 | async-start | bytes 1048576 | tf_op jit(solution)/shard_map/all_to_all | solution.py:34
  387.4 0.3 fusion.7
  387.7 16.0 %all-to-all-done.3 = bf16[16,1,1,2,8192]{4,3,2,1,0:T(2,128)(2,1)S(1)} async-done(((bf16[16,1,1,2,8192]{4,3,2,1,0:T(2,128)(2,1)}), bf16[16,1,1,2,8192]{4,3,2,1,0:T(2,128)(2,1)S(1)}, u32[]{:S(2)}, u32[]{:S(2)}) %all-to-all-start.3) | async-done | bytes 524320 | tf_op jit(solution)/shard_map/all_to_all | solution.py:34
  403.7 0.6 convert_reduce_fusion
  404.3 1.6 fusion.2
  (29 shorter events, 0.6 us)
Async XLA Ops:
  6.5 44.1 %copy-start = (bf16[512,512]{1,0:T(8,128)(2,1)S(1)}, bf16[512,512]{1,0:T(8,128)(2,1)}, u32[]{:S(2)}) copy-start(bf16[512,512]{1,0:T(8,128)(2,1)} %param.11) | copy-start | bytes 1572868
  6.5 44.1 %all-gather.3.cloned.1.call-start = ((), (), s32[]{:S(2)}) async-start(), calls=%async_computation.5 | async-start | bytes 2228224 | tf_op jit(solution)/shard_map/all_gather | solution.py:49
  7.3 55.2 %copy-start.4 = (s32[8]{0:T(128)S(1)}, s32[8]{0:T(128)}, u32[]{:S(2)}) copy-start(s32[8]{0:T(128)} %param.17) | copy-start | bytes 100
  7.3 55.2 %copy-start.5 = (s32[8]{0:T(128)S(1)}, s32[8]{0:T(128)}, u32[]{:S(2)}) copy-start(s32[8]{0:T(128)} %param.16) | copy-start | bytes 100
  55.4 71.8 %copy-start.3 = (bf16[8192]{0:T(1024)(128)(2,1)S(1)}, bf16[8192]{0:T(1024)(128)(2,1)}, u32[]{:S(2)}) copy-start(bf16[8192]{0:T(1024)(128)(2,1)} %param.12) | copy-start | bytes 49156
  55.4 82.6 %copy-start.2 = (bf16[8,8192]{1,0:T(8,128)(2,1)S(1)}, bf16[8,8192]{1,0:T(8,128)(2,1)}, u32[]{:S(2)}) copy-start(bf16[8,8192]{1,0:T(8,128)(2,1)} %param.9) | copy-start | bytes 393220
  55.4 63.5 %all-to-all-start = ((f32[16,128,512]{2,1,0:T(8,128)}), f32[16,128,512]{2,1,0:T(8,128)}, u32[]{:S(2)}, u32[]{:S(2)}) async-start(f32[16,128,512]{2,1,0:T(8,128)} %fusion.20), calls=%async_computation | async-start | bytes 8388608 | tf_op jit(solution)/shard_map/all_to_all | solution.py:18
  122.3 15.8 %all-to-all-start.1 = ((f32[16,8,512]{2,1,0:T(8,128)}), f32[16,8,512]{2,1,0:T(8,128)S(1)}, u32[]{:S(2)}, u32[]{:S(2)}) async-start(f32[16,8,512]{2,1,0:T(8,128)} %bitcast.2), calls=%async_computation.1 | async-start | bytes 524288 | tf_op jit(solution)/shard_map/all_to_all | solution.py:54
  127.2 113.9 %all-gather.5.cloned.1.call-start = ((), (), s32[]{:S(2)}) async-start(), calls=%async_computation.6 | async-start | bytes 8912896 | tf_op jit(solution)/shard_map/all_gather | solution.py:92
  160.1 217.3 %reduce-scatter.2.cloned.1.call-start = ((), (), s32[]{:S(2)}) async-start(), calls=%async_computation.7 | async-start | bytes 17825792 | tf_op jit(solution)/shard_map/reduce_scatter | solution.py:97
  261.7 125.7 %copy-start.1 = (bf16[2,4,8192]{2,1,0:T(4,128)(2,1)S(1)}, bf16[2,4,8192]{2,1,0:T(4,128)(2,1)}, u32[]{:S(2)}) copy-start(bf16[2,4,8192]{2,1,0:T(4,128)(2,1)} %param.13) | copy-start | bytes 393220
  379.8 23.9 %all-to-all-start.3 = ((bf16[16,1,1,2,8192]{4,3,2,1,0:T(2,128)(2,1)}), bf16[16,1,1,2,8192]{4,3,2,1,0:T(2,128)(2,1)S(1)}, u32[]{:S(2)}, u32[]{:S(2)}) async-start(bf16[16,1,1,2,8192]{4,3,2,1,0:T(2,128)(2,1)} %bitcast.15), calls=%async_computation.4 | async-start | bytes 1048576 | tf_op jit(solution)/shard_map/all_to_all | solution.py:34
Sparse Core Ops, SparseCore 0:
  9.2 41.4 all-gather.2
  160.3 80.7 all-gather.4
  261.9 115.4 reduce-scatter.1
where the time goes:
time: 413 us; the launch traced here: 412 us
  waiting for transfers between devices  324 us (78%)
  matrix products  27.6 us (7%)
  blocking collectives  19.8 us (5%)
  starting transfers between devices  19.6 us (5%)
  between operations  13.2 us (3%)
  other arithmetic  5.66 us (1%)
    reduce_scatter x1, waiting for transfers between devices, per_device(): lax.psum_scatter(jnp.dot(hidden, down_matrix, preferred_element_type=jnp....  116 us
    all_gather x1, waiting for transfers between devices, per_device(): lax.all_gather(local_slots, 'tp', axis=0, tiled=True)  80.9 us
    all_to_all x1, waiting for transfers between devices, summed_on_arrival(): lax.all_to_all(in_blocks(array, dim, length), axis, 0, 0, tiled=True)  56.5 us
    all_gather x1, waiting for transfers between devices, per_device(): all_rows = lax.all_gather(grouped, ('role', 'exp'), axis=1, tiled=True)  43.4 us
    all_to_all x1, blocking collectives, joined_exchange(): lax.all_to_all(blocks, axis, split_axis=0, concat_axis=0, tiled=True)  19.8 us
    all_to_all x1, waiting for transfers between devices, joined_exchange(): lax.all_to_all(blocks, axis, split_axis=0, concat_axis=0, tiled=True)  16 us
    dot_general x1, matrix products, per_device(): jnp.dot(hidden, down_matrix, preferred_element_type=jnp.float32)  10.9 us
    all_to_all x1, waiting for transfers between devices, per_device(): lax.all_to_all(partial_cols.reshape(group_count, tok_rows, out_weight.sha...  10.6 us
  transfers between devices with their start and end apart: 6, of which 6 were waited for; matrix products, arithmetic and copies ran while one was open for 0% of the time, Pallas kernels for 0%

commit v1 on v0

--- a/solution.py
+++ b/solution.py
@@ -6,6 +6,15 @@
 EXPERTS = 4
 CAP = 2
 EPSILON = 1e-05
+
+
+def _save_ladders(local, ax_name):
+    return jnp.concatenate(
+        lax.all_to_all(
+            jnp.stack(lax.axis_size(ax_name) * [local], 0), ax_name, split_axis=0, concat_axis=0
+        ),
+        0,
+    )
 
 
 def in_blocks(array, dim, length):
@@ -89,9 +98,7 @@
     up_matrix = up_weight[0, 0]
     down_matrix = down_weight[0, 0]
     up_sums = jnp.dot(
-        lax.all_gather(local_slots, "tp", axis=0, tiled=True),
-        up_matrix,
-        preferred_element_type=jnp.float32,
+        _save_ladders(local_slots, "tp"), up_matrix, preferred_element_type=jnp.float32
     )
     hidden = jax.nn.gelu(up_sums).astype(jnp.bfloat16)
     results = lax.psum_scatter(

time: 413 us -> 434 us (1.051)
  blocking collectives: 19.8 us -> 129 us
  waiting for transfers between devices: 324 us -> 241 us
  matrix products: 27.6 us -> 22.6 us
    all_to_all x0 -> x1, blocking collectives: none -> 109 us  [_save_ladders(): lax.all_to_all(jnp.stack(lax.axis_size(ax_name) * [local], 0), ax_name, s...]
    all_gather x1 -> x0, waiting for transfers between devices: 80.9 us -> none  [per_device(): lax.all_gather(local_slots, 'tp', axis=0, tiled=True)]
  transfers between devices with their start and end apart: 6 -> 5, of which waited for: 6 -> 5; matrix products, arithmetic and copies ran while one was open for 0% -> 0% of each run, Pallas kernels for 0% -> 0%
where the time goes in v1:
time: 434 us
  waiting for transfers between devices  241 us (56%)
  blocking collectives  129 us (30%)
  matrix products  22.6 us (5%)
  starting transfers between devices  19.4 us (4%)
  between operations  13.6 us (3%)
  other arithmetic  5.65 us (1%)
    reduce_scatter x1, waiting for transfers between devices, per_device(): lax.psum_scatter(jnp.dot(hidden, down_matrix, preferred_element_type=jnp....  114 us
    all_to_all x1, blocking collectives, _save_ladders(): lax.all_to_all(jnp.stack(lax.axis_size(ax_name) * [local], 0), ax_name, s...  109 us
    all_to_all x1, waiting for transfers between devices, summed_on_arrival(): lax.all_to_all(in_blocks(array, dim, length), axis, 0, 0, tiled=True)  56.5 us
    all_gather x1, waiting for transfers between devices, per_device(): all_rows = lax.all_gather(grouped, ('role', 'exp'), axis=1, tiled=True)  43.4 us
    all_to_all x1, blocking collectives, joined_exchange(): lax.all_to_all(blocks, axis, split_axis=0, concat_axis=0, tiled=True)  19.8 us
    all_to_all x1, waiting for transfers between devices, joined_exchange(): lax.all_to_all(blocks, axis, split_axis=0, concat_axis=0, tiled=True)  16 us
    all_to_all x1, waiting for transfers between devices, per_device(): lax.all_to_all(partial_cols.reshape(group_count, tok_rows, out_weight.sha...  10.6 us
  transfers between devices with their start and end apart: 5, of which 5 were waited for; matrix products, arithmetic and copies ran while one was open for 0% of the time, Pallas kernels for 0%

profile of v1, /device:TPU:32, one launch (start us, length us, event | category | flops | bytes accessed | tf_op | source)
XLA Modules:
  0.0 433.6 jit_solution(5413107088751852799)
XLA Ops:
  6.5 0.7 all-gather.2.cloned.1.call-update
  7.3 43.4 %all-gather.2.cloned.1.call-done = bf16[16,128,512]{2,1,0:T(8,128)(2,1)} async-done(((bf16[16,8,512]{2,1,0:T(8,128)(2,1)}), bf16[16,128,512]{2,1,0:T(8,128)(2,1)}) %all-gather.2.cloned.1.call-update) | async-done | bytes 2097168 | tf_op jit(solution)/shard_map/all_gather | solution.py:58
  50.6 4.8 %fusion.20 = f32[16,128,512]{2,1,0:T(8,128)} fusion(bf16[16,128,512]{2,1,0:T(8,128)(2,1)} %all-gather.2.cloned.1.call-done, bf16[512,512]{1,0:T(8,128)(2,1)S(1)} %copy-done), kind=kOutput, calls=%fused_computation.21 | convolution fusion | flops 1073741824 | bytes 6815744 | tf_op jit(solution)/shard_map/dot_general | solution.py:61
  55.4 7.0 %all-to-all-start = ((f32[16,128,512]{2,1,0:T(8,128)}), f32[16,128,512]{2,1,0:T(8,128)}, u32[]{:S(2)}, u32[]{:S(2)}) async-start(f32[16,128,512]{2,1,0:T(8,128)} %fusion.20), calls=%async_computation | async-start | bytes 8388608 | tf_op jit(solution)/shard_map/all_to_all | solution.py:27
  62.5 56.5 %all-to-all-done = f32[16,128,512]{2,1,0:T(8,128)} async-done(((f32[16,128,512]{2,1,0:T(8,128)}), f32[16,128,512]{2,1,0:T(8,128)}, u32[]{:S(2)}, u32[]{:S(2)}) %all-to-all-start) | async-done | bytes 4194336 | tf_op jit(solution)/shard_map/all_to_all | solution.py:27
  119.0 3.3 reduce_sum.45
  122.3 4.9 %all-to-all-start.1 = ((f32[16,8,512]{2,1,0:T(8,128)}), f32[16,8,512]{2,1,0:T(8,128)S(1)}, u32[]{:S(2)}, u32[]{:S(2)}) async-start(f32[16,8,512]{2,1,0:T(8,128)} %bitcast.2), calls=%async_computation.1 | async-start | bytes 524288 | tf_op jit(solution)/shard_map/all_to_all | solution.py:63
  127.4 10.6 %all-to-all-done.1 = f32[16,8,512]{2,1,0:T(8,128)S(1)} async-done(((f32[16,8,512]{2,1,0:T(8,128)}), f32[16,8,512]{2,1,0:T(8,128)S(1)}, u32[]{:S(2)}, u32[]{:S(2)}) %all-to-all-start.1) | async-done | bytes 262176 | tf_op jit(solution)/shard_map/all_to_all | solution.py:63
  138.3 0.3 convolution_convert_fusion
  138.6 0.3 copy.13
  138.9 0.4 broadcast_in_dim.6
  139.3 19.8 %all_to_all.35 = bf16[16,1,1,2,8192]{4,3,2,1,0:T(2,128)(2,1)S(1)} all-to-all(bf16[16,1,1,2,8192]{4,3,2,1,0:T(2,128)(2,1)S(1)} %bitcast.68), channel_id=1, replica_groups=mesh['role'=2,'exp'=8,'tp'=16] {'role','exp'}, dimensions={0} | all-to-all | bytes 1048576 | tf_op jit(solution)/shard_map/all_to_all | solution.py:43
  159.3 1.0 stack.3
  160.3 108.8 %all_to_all.36 = bf16[16,32,8192]{2,1,0:T(8,128)(2,1)S(1)} all-to-all(bf16[16,32,8192]{2,1,0:T(8,128)(2,1)S(1)} %stack.3), channel_id=1, replica_groups=mesh['role'=2,'exp'=8,'tp'=16] {'tp'}, dimensions={0} | all-to-all | bytes 16777216 | tf_op jit(solution)/shard_map/all_to_all | solution.py:13
  269.1 7.5 %fusion.17 = bf16[512,384]{1,0:T(8,128)(2,1)S(1)} fusion(bf16[512,8192]{1,0:T(8,128)(2,1)S(1)} %bitcast.64, bf16[1,1,8192,384]{3,2,1,0:T(8,128)(2,1)} %param.14), kind=kOutput, calls=%fused_computation.20 | convolution fusion | flops 3222994944 | bytes 15073280 | tf_op jit(solution)/shard_map/dot_general | solution.py:100
  276.7 8.1 %fusion.3 = f32[512,8192]{1,0:T(8,128)} fusion(bf16[512,384]{1,0:T(8,128)(2,1)S(1)} %fusion.17, bf16[1,1,384,8192]{3,2,1,0:T(8,128)(2,1)S(1)} %bitcast.66), kind=kOutput, calls=%fused_computation.5 | convolution fusion | flops 3221225472 | bytes 23461888 | tf_op jit(solution)/shard_map/dot_general | solution.py:105
  284.8 113.6 %reduce-scatter.2.cloned.1.call-done = f32[32,8192]{1,0:T(8,128)} async-done(((f32[512,8192]{1,0:T(8,128)}), f32[32,8192]{1,0:T(8,128)}) %reduce-scatter.2.cloned.1.call-update) | async-done | bytes 1048592 | tf_op jit(solution)/shard_map/reduce_scatter | solution.py:104
  398.3 1.3 convert_element_type.70
  399.6 1.1 convert_element_type.71
  400.7 7.5 %all-to-all-start.4 = ((bf16[16,1,1,2,8192]{4,3,2,1,0:T(2,128)(2,1)}), bf16[16,1,1,2,8192]{4,3,2,1,0:T(2,128)(2,1)S(1)}, u32[]{:S(2)}, u32[]{:S(2)}) async-start(bf16[16,1,1,2,8192]{4,3,2,1,0:T(2,128)(2,1)} %bitcast.16), calls=%async_computation.5 | async-start | bytes 1048576 | tf_op jit(solution)/shard_map/all_to_all | solution.py:43
  408.3 0.3 fusion.7
  408.6 16.0 %all-to-all-done.4 = bf16[16,1,1,2,8192]{4,3,2,1,0:T(2,128)(2,1)S(1)} async-done(((bf16[16,1,1,2,8192]{4,3,2,1,0:T(2,128)(2,1)}), bf16[16,1,1,2,8192]{4,3,2,1,0:T(2,128)(2,1)S(1)}, u32[]{:S(2)}, u32[]{:S(2)}) %all-to-all-start.4) | async-done | bytes 524320 | tf_op jit(solution)/shard_map/all_to_all | solution.py:43
  424.6 0.6 convert_reduce_fusion
  425.2 1.6 fusion.2
  (33 shorter events, 0.8 us)
Async XLA Ops:
  6.5 44.1 %copy-start = (bf16[512,512]{1,0:T(8,128)(2,1)S(1)}, bf16[512,512]{1,0:T(8,128)(2,1)}, u32[]{:S(2)}) copy-start(bf16[512,512]{1,0:T(8,128)(2,1)} %param.11) | copy-start | bytes 1572868
  6.5 44.1 %all-gather.2.cloned.1.call-start = ((), (), s32[]{:S(2)}) async-start(), calls=%async_computation.6 | async-start | bytes 2228224 | tf_op jit(solution)/shard_map/all_gather | solution.py:58
  7.3 55.2 %copy-start.4 = (s32[8]{0:T(128)S(1)}, s32[8]{0:T(128)}, u32[]{:S(2)}) copy-start(s32[8]{0:T(128)} %param.17) | copy-start | bytes 100
  7.3 55.2 %copy-start.5 = (s32[8]{0:T(128)S(1)}, s32[8]{0:T(128)}, u32[]{:S(2)}) copy-start(s32[8]{0:T(128)} %param.16) | copy-start | bytes 100
  55.4 71.8 %copy-start.3 = (bf16[8192]{0:T(1024)(128)(2,1)S(1)}, bf16[8192]{0:T(1024)(128)(2,1)}, u32[]{:S(2)}) copy-start(bf16[8192]{0:T(1024)(128)(2,1)} %param.12) | copy-start | bytes 49156
  55.4 82.6 %copy-start.2 = (bf16[8,8192]{1,0:T(8,128)(2,1)S(1)}, bf16[8,8192]{1,0:T(8,128)(2,1)}, u32[]{:S(2)}) copy-start(bf16[8,8192]{1,0:T(8,128)(2,1)} %param.9) | copy-start | bytes 393220
  55.4 63.5 %all-to-all-start = ((f32[16,128,512]{2,1,0:T(8,128)}), f32[16,128,512]{2,1,0:T(8,128)}, u32[]{:S(2)}, u32[]{:S(2)}) async-start(f32[16,128,512]{2,1,0:T(8,128)} %fusion.20), calls=%async_computation | async-start | bytes 8388608 | tf_op jit(solution)/shard_map/all_to_all | solution.py:27
  122.3 15.8 %all-to-all-start.1 = ((f32[16,8,512]{2,1,0:T(8,128)}), f32[16,8,512]{2,1,0:T(8,128)S(1)}, u32[]{:S(2)}, u32[]{:S(2)}) async-start(f32[16,8,512]{2,1,0:T(8,128)} %bitcast.2), calls=%async_computation.1 | async-start | bytes 524288 | tf_op jit(solution)/shard_map/all_to_all | solution.py:63
  127.2 271.2 %reduce-scatter.2.cloned.1.call-start = ((), (), s32[]{:S(2)}) async-start(), calls=%async_computation.7 | async-start | bytes 17825792 | tf_op jit(solution)/shard_map/reduce_scatter | solution.py:104
  160.3 116.3 %slice-start = ((s8[6291456]{0:T(1024)(128)(4,1)}), s8[4194304]{0:T(1024)(128)(4,1)S(1)}, s32[]{:S(2)}) async-start(s8[6291456]{0:T(1024)(128)(4,1)} %bitcast.65), calls=%async_computation.8 | async-start | bytes 8388608
  269.1 7.6 %slice-start.1 = ((s8[6291456]{0:T(1024)(128)(4,1)}), s8[2097152]{0:T(1024)(128)(4,1)S(1)}, s32[]{:S(2)}) async-start(s8[6291456]{0:T(1024)(128)(4,1)} %bitcast.65), calls=%async_computation.9 | async-start | bytes 4194304
  284.7 123.5 %copy-start.1 = (bf16[2,4,8192]{2,1,0:T(4,128)(2,1)S(1)}, bf16[2,4,8192]{2,1,0:T(4,128)(2,1)}, u32[]{:S(2)}) copy-start(bf16[2,4,8192]{2,1,0:T(4,128)(2,1)} %param.13) | copy-start | bytes 393220
  400.7 23.8 %all-to-all-start.4 = ((bf16[16,1,1,2,8192]{4,3,2,1,0:T(2,128)(2,1)}), bf16[16,1,1,2,8192]{4,3,2,1,0:T(2,128)(2,1)S(1)}, u32[]{:S(2)}, u32[]{:S(2)}) async-start(bf16[16,1,1,2,8192]{4,3,2,1,0:T(2,128)(2,1)} %bitcast.16), calls=%async_computation.5 | async-start | bytes 1048576 | tf_op jit(solution)/shard_map/all_to_all | solution.py:43
Sparse Core Ops, SparseCore 0:
  9.2 41.4 all-gather.1
  284.9 113.4 reduce-scatter.1
